TPU v7x, 512 devices: a whole 4x4x16 slice. The times are simulated.
512 devices in a mesh: band: 8 (over x_lo, y), lon: 64 (over x_hi, z, core).
Axes of the slice: x: 4 (x_hi: 2, x_lo: 2; x = x_hi * 2 + x_lo), y: 4, z: 16, core: 2. Of those that a mesh axis runs over, the one named last changes fastest.
Arguments:
- tracers: float32 [384, 1024, 128], P('band', 'lon'), may hold values from -6 to 6
- lon_offset: int32 [384, 4], P('band'), may hold values from -512 to 511
- lon_weights: float32 [4, 384, 4], P(None, 'band'), may hold values from -0.1 to 1, as said below
- lat_offset: int32 [384, 4], P('band'), may hold values from -6 to 6
- lat_weights: float32 [4, 384, 4], P(None, 'band'), may hold values from -0.1 to 1, as said below
Outputs:
- advected: float32 [384, 1024, 128], P('band', 'lon')
Inputs may be any that keep to these rules, and one draw needn't show every extreme that they name: `lon_weights`: each set of four weights sums to one. `lat_weights`: each set of four weights sums to one.
All inputs are finite; a program needn't handle non-finite values.
Results may differ from a plain program's by a relative error of at most 0.0003.
Values sent between devices are 32-bit elements; how exact they have to be, the bound alone decides.
No kernel may reach another device: no remote copies, remote signals or barrier semaphores. Data moves between devices by JAX's collectives and lax.ppermute only.
A program may use at most 64 MiB of HBM per device.

v0:
```python
import functools

import jax
import jax.numpy as jnp
from jax import lax
from jax.experimental import pallas as pl
from jax.experimental.pallas import tpu as pltpu
from jax.sharding import PartitionSpec as P


REACH = 8
PARTS = 1
VMEM = pltpu.VMEM
SMEM = pltpu.SMEM
DMA = pltpu.SemaphoreType.DMA
PARAMS = pltpu.CompilerParams(vmem_limit_bytes=8 * 1024 * 1024)


def columns_first(block, groups):
    return block.T.reshape(groups, block.shape[1] // groups, block.shape[0])


def rows_first(slab):
    return slab.reshape(slab.shape[0] * slab.shape[1], slab.shape[2]).T


def split_kernel(x_ref, *refs):
    count = (len(refs) - 4) // 2
    o_ref = refs[count]
    in_ref, x_sem, t_sem = refs[-3:]
    pairs, cores, slabs, sets, per_set, _ = o_ref.shape
    part = x_ref.shape[0] // PARTS
    copies = []
    for i in range(PARTS):
        block = pl.ds(i * part, part)
        copies.append(pltpu.make_async_copy(x_ref.at[block], in_ref.at[block], x_sem.at[i]))
        copies[-1].start()
    tables = []
    for i in range(count):
        tables.append(pltpu.make_async_copy(refs[i], refs[count + 1 + i], t_sem.at[i]))
        tables[-1].start()
    for i in range(cores * slabs):
        if i * 128 % part == 0:
            copies[i * 128 // part].wait()
        value = columns_first(in_ref[i * 128 : (i + 1) * 128, :], pairs * sets).reshape(pairs, sets, per_set, 128)
        o_ref[:, i // slabs, i % slabs] = value
    for copy in tables:
        copy.wait()


def last_kernel(x_ref, o_ref, out_ref, sem):
    pairs, cores, slabs, sets, per_set, _ = x_ref.shape
    copies = []
    for i in range(cores * slabs):
        block = pl.ds(i * 128, 128)
        value = x_ref[:, i // slabs, i % slabs].reshape(pairs * sets, per_set, 128)
        out_ref[i * 128 : (i + 1) * 128, :] = rows_first(value)
        copies.append(pltpu.make_async_copy(out_ref.at[block], o_ref.at[block], sem.at[i]))
        copies[-1].start()
    for copy in copies:
        copy.wait()


def placed(lines, offset, ext_refs, cells, lanes_per_block):
    lanes = lines[0].shape[1]
    circle = lanes // lanes_per_block * cells
    wrapped = offset & (circle - 1)
    step = (wrapped >> (cells.bit_length() - 1)) * lanes_per_block
    before = (step + lanes_per_block) & (lanes - 1)
    after = (step + lanes - lanes_per_block) & (lanes - 1)
    for line, ext_ref in zip(lines, ext_refs):
        ext_ref[0:cells] = pltpu.roll(line, before, 1)
        ext_ref[cells : 2 * cells] = pltpu.roll(line, step, 1)
        ext_ref[2 * cells : 2 * cells + 8] = pltpu.roll(line[0:8], after, 1)
    return cells - 1 - (wrapped & (cells - 1))


def tapped(start, weights, ext_refs, cells):
    totals = []
    for ext_ref in ext_refs:
        total = None
        for k in range(4):
            term = weights[k] * ext_ref[pl.ds(start + k, cells), :]
            total = term if total is None else total + term
        totals.append(total)
    return totals


def here(levels):
    lon = lax.axis_index("lon")
    return lax.div(lon * levels, lax.axis_size("lon")), lax.rem(lon, 2)


def first_pass(x_ref, slab, row, level, off_ref, w_ref, o_ref, turn_ref, ext_ref, cells):
    sets, per_set = x_ref.shape[2:4]
    for g in range(sets):
        turn_ref[g] = rows_first(x_ref[:, slab, g])
    count = 128 // cells
    exts = [[ext_ref[i].at[g] for g in range(sets)] for i in range(count)]
    starts = []
    for i in range(count):
        lines = [turn_ref[g, i * cells : (i + 1) * cells, :] for g in range(sets)]
        starts.append(placed(lines, off_ref[level, row + i], exts[i], cells, per_set))
    for i in range(count):
        values = tapped(starts[i], [w_ref[k, level, row + i] for k in range(4)], exts[i], cells)
        for g in range(sets):
            o_ref[g * 128 + i * cells : g * 128 + (i + 1) * cells, :] = values[g]


def rows_done(slab, half, window_ref, first_place, level, core, tables, o_ref, turn_ref, ext_ref, cells, use=1):
    off_ref, w_ref, toff_ref, tw_ref = tables
    groups, _, sets, per_set, _ = o_ref.shape
    rows = 2 * half
    per_slab = 128 // cells
    first_row = lax.axis_index("band") * rows
    last_row = lax.axis_size("band") * rows - 1
    half_row = core * half
    first = half_row + slab * per_slab
    exts = [[ext_ref[use * per_slab + i].at[g] for g in range(sets)] for i in range(per_slab)]
    starts = []
    for i in range(per_slab):
        row = first + i
        shift = toff_ref[level, row]
        totals = [None] * sets
        for k in range(4):
            source = jnp.clip(first_row + row + (k - 1) - shift, 0, last_row) - first_row - half_row - first_place
            weight = tw_ref[k, level, row]
            where = pl.ds(pl.multiple_of(source * cells, cells), cells)
            for g in range(sets):
                term = weight * window_ref[g, where, :]
                totals[g] = term if totals[g] is None else totals[g] + term
        starts.append(placed(totals, off_ref[level, row], exts[i], cells, per_set))
    for i in range(per_slab):
        values = tapped(starts[i], [w_ref[k, level, first + i] for k in range(4)], exts[i], cells)
        for g in range(sets):
            turn_ref[g, i * cells : (i + 1) * cells, :] = values[g]
    for g in range(sets):
        o_ref[:, slab, g] = columns_first(turn_ref[g], groups)


def edge_kernel(cells, levels, half, far, x_ref, off_ref, w_ref, o_ref, turn_ref, ext_ref):
    level, core = here(levels)
    slab = (core if far else 1 - core) * (x_ref.shape[1] - 1)
    row = core * half + slab * (128 // cells)
    first_pass(x_ref, slab, row, level, off_ref, w_ref, o_ref, turn_ref, ext_ref, cells)


def inner_kernel(
    cells, levels, half, x_ref, far_ref, near_ref, halo_ref, off_ref, w_ref, toff_ref, tw_ref, o_ref, mid_ref, own_ref, turn_ref, ext_ref
):
    level, core = here(levels)
    sets = x_ref.shape[2]
    row = core * half + 128 // cells
    first_pass(x_ref, 1, row, level, off_ref, w_ref, mid_ref, turn_ref, ext_ref, cells)
    for g in range(sets):
        part = slice(g * 128, (g + 1) * 128)
        own_ref[g, pl.ds(pl.multiple_of(128 + core * 256, 128), 128), :] = far_ref[part, :]
        own_ref[g, 256:384, :] = mid_ref[part, :]
        own_ref[g, pl.ds(pl.multiple_of(384 - core * 256, 128), 128), :] = near_ref[part, :]
        own_ref[g, pl.ds(pl.multiple_of(512 - core * 512, 128), 128), :] = halo_ref[1 - core, part, :]
    tables = (off_ref, w_ref, toff_ref, tw_ref)
    for use, slab in ((1, 1), (2, 2 - 2 * core)):
        rows_done(slab, half, own_ref, -(128 // cells), level, core, tables, o_ref, turn_ref, ext_ref, cells, use)


def outer_kernel(
    cells, levels, half, edge_ref, mid_ref, halo_ref, off_ref, w_ref, toff_ref, tw_ref, i_ref, o_ref, own_ref, turn_ref, ext_ref
):
    level, core = here(levels)
    for g in range(o_ref.shape[2]):
        part = slice(g * 128, (g + 1) * 128)
        own_ref[g, pl.ds(pl.multiple_of(core * 256, 128), 128), :] = halo_ref[part, :]
        own_ref[g, 128:256, :] = edge_ref[part, :]
        own_ref[g, pl.ds(pl.multiple_of((1 - core) * 256, 128), 128), :] = mid_ref[part, :]
    slab = core * 2
    first_place = (slab - 1) * (128 // cells)
    tables = (off_ref, w_ref, toff_ref, tw_ref)
    rows_done(slab, half, own_ref, first_place, level, core, tables, o_ref, turn_ref, ext_ref, cells)


def exchanged(x):
    return lax.all_to_all(x, "lon", 0, 0, tiled=True)


def per_device(tracers, lon_offset, lon_weights, lat_offset, lat_weights):
    rows, cells, columns = tracers.shape
    levels = lon_offset.shape[1]
    groups = lax.axis_size("lon")
    bands = lax.axis_size("band")
    flat = rows * cells
    half = rows // 2
    slabs = half * cells // 128
    per_set = 128 // groups
    sets = columns * 2 // groups // per_set
    f32 = jnp.float32
    vspec = pl.BlockSpec(memory_space=VMEM)
    sspec = pl.BlockSpec(memory_space=SMEM)
    hspec = pl.BlockSpec(memory_space=pltpu.HBM)
    tables = (lon_offset.T, lon_weights.transpose(0, 2, 1), lat_offset.T, lat_weights.transpose(0, 2, 1))
    assert slabs == 3 and REACH * cells == 128 and columns == 128
    sent = jax.ShapeDtypeStruct((groups // 2, 2, slabs, sets, per_set, 128), f32)
    slab_lines = jax.ShapeDtypeStruct((sets * 128, 128), f32)
    gathered_shape = (groups, *sent.shape[2:])
    turn = VMEM((sets, 128, 128), f32)
    ext = (VMEM((sets, 2 * cells + 8, 128), f32),) * (3 * 128 // cells)
    own = VMEM((sets, 3 * 128, 128), f32)

    def call(kernel, out_shape, in_specs, scratch, *args, aliases={}):
        return pl.pallas_call(
            kernel,
            out_shape=out_shape,
            in_specs=in_specs,
            out_specs=jax.tree.map(lambda x: vspec if isinstance(x, jax.ShapeDtypeStruct) else sspec, out_shape),
            scratch_shapes=scratch,
            input_output_aliases=aliases,
            compiler_params=PARAMS,
        )(*args)

    given = [pltpu.with_memory_space_constraint(x, pltpu.HBM) for x in (tracers.reshape(flat, columns), *tables)]
    spread, *tables = call(
        split_kernel,
        [sent] + [SMEM(x.shape, x.dtype) for x in tables],
        [hspec] * 5,
        [VMEM((flat, columns), f32), DMA((PARTS,)), DMA((4,))],
        *given,
    )
    tables = [pltpu.with_memory_space_constraint(x, SMEM) for x in tables]
    gathered = exchanged(spread.reshape(gathered_shape))

    def edge(far):
        kernel = functools.partial(edge_kernel, cells, levels, half, far)
        return call(kernel, slab_lines, [vspec, sspec, sspec], [turn, ext], gathered, *tables[:2])

    far = edge(True)
    pairs = []
    for n in range(bands - 1):
        for lon in range(1, groups, 2):
            lower, upper = n * groups + lon, (n + 1) * groups + lon - 1
            pairs += [(lower, upper), (upper, lower)]
    far_halo = lax.ppermute(far, ("band", "lon"), pairs)
    near = edge(False)
    near_halo = lax.all_gather(near, "lon", axis_index_groups=[[lon, lon + 1] for lon in range(0, groups, 2)])
    out, mid = call(
        functools.partial(inner_kernel, cells, levels, half),
        [jax.ShapeDtypeStruct(gathered_shape, f32), slab_lines],
        [vspec] * 4 + [sspec] * 4,
        [VMEM((sets, 5 * 128, 128), f32), turn, ext],
        gathered,
        far,
        near,
        near_halo,
        *tables,
    )
    out = call(
        functools.partial(outer_kernel, cells, levels, half),
        jax.ShapeDtypeStruct(gathered_shape, f32),
        [vspec] * 3 + [sspec] * 4 + [vspec],
        [own, turn, ext],
        far,
        mid,
        far_halo,
        *tables,
        out,
        aliases={7: 0},
    )
    last = pl.pallas_call(
        last_kernel,
        out_shape=jax.ShapeDtypeStruct((flat, columns), f32),
        in_specs=[vspec],
        out_specs=hspec,
        scratch_shapes=[VMEM((flat, columns), f32), DMA((flat // 128,))],
        compiler_params=PARAMS,
        name="last",
    )(exchanged(out).reshape(sent.shape))
    return last.reshape(rows, cells, columns)


def solution(mesh):
    return jax.shard_map(
        per_device,
        mesh=mesh,
        in_specs=(
            P("band", "lon", None),
            P("band", None),
            P(None, "band", None),
            P("band", None),
            P(None, "band", None),
        ),
        out_specs=P("band", "lon", None),
        check_vma=False,
    )
```

profile of v0, /device:TPU:25, one launch (start us, length us, event | category | flops | bytes accessed | tf_op | source)
XLA Modules:
  0.0 91.4 jit_solution(15725670444472543144)
XLA Ops:
  0.0 1.2 %shard_map.55 = (f32[32,2,3,2,2,128]{5,4,3,2,1,0:T(2,128)S(1)}, s32[4,48]{1,0:T(4,128)S(4)}, f32[4,4,48]{2,1,0:T(4,128)S(4)}, s32[4,48]{1,0:T(4,128)S(4)}, f32[4,4,48]{2,1,0:T(4,128)S(4)}) custom-call(f32[768,128]{1,0:T(8,128)} %bitcast.12, s32[4,48]{1,0:T(4,128)} %bitcast.15, f32[4,4,48]{2,1,0:T(4,128)} %bitcast.13, s32[4,48]{1,0:T(4,128)} %bitcast.16, ...), custom_call_target="tpu_custom_call" | custom-call | tf_op jit(solution)/shard_map/pallas_call | solution.py:209
  1.3 47.4 %all_to_all.10.x_ref = f32[64,3,2,2,128]{4,3,2,1,0:T(2,128)S(1)} all-to-all(f32[64,3,2,2,128]{4,3,2,1,0:T(2,128)S(1)} %bitcast.11), channel_id=1, replica_groups=mesh['band'=8,'lon'=64] {'lon'}, dimensions={0} | all-to-all | bytes 786432 | tf_op jit(solution)/shard_map/all_to_all | solution.py:182
  48.6 0.2 shard_map.56.far_ref.edge_ref
  48.9 1.9 %collective-permute-start = (f32[256,128]{1,0:T(8,128)S(1)}, f32[256,128]{1,0:T(8,128)S(1)}, u32[]{:S(2)}, u32[]{:S(2)}) collective-permute-start(f32[256,128]{1,0:T(8,128)S(1)} %shard_map.56.far_ref.edge_ref), channel_id=1, source_target_pairs={{1,64},{64,1},{3,66},{66,3},{5,68},{68,5},{7,70},{70,7},{9,72},{72... | collective-permute-start | bytes 393224 | tf_op jit(solution)/shard_map/ppermute | solution.py:240
  50.8 0.3 shard_map.57.near_ref
  51.1 2.5 %all-gather = f32[512,128]{1,0:T(8,128)S(1)} all-gather(f32[256,128]{1,0:T(8,128)S(1)} %shard_map.57.near_ref), channel_id=2, replica_groups={{0,1},{2,3},{4,5},{6,7},{8,9},{10,11},{12,13},{14,15},{16,17},{18,19},{..., dimensions={0}, use_global_device_ids=true | all-gather | bytes 393216 | tf_op jit(solution)/shard_map/all_gather | solution.py:242
  53.6 0.8 shard_map.58
  54.3 3.0 %collective-permute-done.halo_ref = f32[256,128]{1,0:T(8,128)S(1)} collective-permute-done((f32[256,128]{1,0:T(8,128)S(1)}, f32[256,128]{1,0:T(8,128)S(1)}, u32[]{:S(2)}, u32[]{:S(2)}) %collective-permute-start) | collective-permute-done | bytes 131104 | tf_op jit(solution)/shard_map/ppermute | solution.py:240
  57.3 0.4 shard_map.59
  57.7 32.8 %all_to_all.11 = f32[64,3,2,2,128]{4,3,2,1,0:T(2,128)S(1)} all-to-all(f32[64,3,2,2,128]{4,3,2,1,0:T(2,128)S(1)} %shard_map.59), channel_id=1, replica_groups=mesh['band'=8,'lon'=64] {'lon'}, dimensions={0} | all-to-all | bytes 786432 | tf_op jit(solution)/shard_map/all_to_all | solution.py:182
  90.5 0.9 last.1
Async XLA Ops:
  48.9 8.4 %collective-permute-start = (f32[256,128]{1,0:T(8,128)S(1)}, f32[256,128]{1,0:T(8,128)S(1)}, u32[]{:S(2)}, u32[]{:S(2)}) collective-permute-start(f32[256,128]{1,0:T(8,128)S(1)} %shard_map.56.far_ref.edge_ref), channel_id=1, source_target_pairs={{1,64},{64,1},{3,66},{66,3},{5,68},{68,5},{7,70},{70,7},{9,72},{72... | collective-permute-start | bytes 393224 | tf_op jit(solution)/shard_map/ppermute | solution.py:240
where the time goes:
time: 91.6 us; the launch traced here: 91.4 us
  blocking collectives  82.7 us (90%)
  Pallas kernels  3.76 us (4%)
  waiting for transfers between devices  2.97 us (3%)
  starting transfers between devices  1.92 us (2%)
    all_to_all x2, blocking collectives, exchanged(): return lax.all_to_all(x, 'lon', 0, 0, tiled=True)  80.2 us
    ppermute x1, waiting for transfers between devices, per_device(): far_halo = lax.ppermute(far, ('band', 'lon'), pairs)  2.97 us
    pallas_call x5, Pallas kernels, call(): pl.pallas_call(kernel, out_shape=out_shape, in_specs=in_specs, out_specs=...  2.86 us
    all_gather x1, blocking collectives, per_device(): lax.all_gather(near, 'lon', axis_index_groups=[[lon, lon + 1] for lon in...  2.47 us
    ppermute x1, starting transfers between devices, per_device(): far_halo = lax.ppermute(far, ('band', 'lon'), pairs)  1.92 us
  transfers between devices with their start and end apart: 1, of which 1 were waited for; matrix products, arithmetic and copies ran while one was open for 0% of the time, Pallas kernels for 1%

commit v1 on v0

--- a/solution.py
+++ b/solution.py
@@ -28,7 +28,7 @@
     count = (len(refs) - 4) // 2
     o_ref = refs[count]
     in_ref, x_sem, t_sem = refs[-3:]
-    pairs, cores, slabs, sets, per_set, _ = o_ref.shape
+    pairs, cores, slabs, _, _ = o_ref.shape
     part = x_ref.shape[0] // PARTS
     copies = []
     for i in range(PARTS):
@@ -42,19 +42,17 @@
     for i in range(cores * slabs):
         if i * 128 % part == 0:
             copies[i * 128 // part].wait()
-        value = columns_first(in_ref[i * 128 : (i + 1) * 128, :], pairs * sets).reshape(pairs, sets, per_set, 128)
-        o_ref[:, i // slabs, i % slabs] = value
+        o_ref[:, i // slabs, i % slabs] = columns_first(in_ref[i * 128 : (i + 1) * 128, :], pairs)
     for copy in tables:
         copy.wait()
 
 
 def last_kernel(x_ref, o_ref, out_ref, sem):
-    pairs, cores, slabs, sets, per_set, _ = x_ref.shape
+    _, cores, slabs, _, _ = x_ref.shape
     copies = []
     for i in range(cores * slabs):
         block = pl.ds(i * 128, 128)
-        value = x_ref[:, i // slabs, i % slabs].reshape(pairs * sets, per_set, 128)
-        out_ref[i * 128 : (i + 1) * 128, :] = rows_first(value)
+        out_ref[i * 128 : (i + 1) * 128, :] = rows_first(x_ref[:, i // slabs, i % slabs])
         copies.append(pltpu.make_async_copy(out_ref.at[block], o_ref.at[block], sem.at[i]))
         copies[-1].start()
     for copy in copies:
@@ -92,9 +90,10 @@
 
 
 def first_pass(x_ref, slab, row, level, off_ref, w_ref, o_ref, turn_ref, ext_ref, cells):
-    sets, per_set = x_ref.shape[2:4]
+    per_set = turn_ref.shape[2] // x_ref.shape[0]
+    sets = x_ref.shape[2] // per_set
     for g in range(sets):
-        turn_ref[g] = rows_first(x_ref[:, slab, g])
+        turn_ref[g] = rows_first(x_ref[:, slab, g * per_set : (g + 1) * per_set])
     count = 128 // cells
     exts = [[ext_ref[i].at[g] for g in range(sets)] for i in range(count)]
     starts = []
@@ -109,7 +108,9 @@
 
 def rows_done(slab, half, window_ref, first_place, level, core, tables, o_ref, turn_ref, ext_ref, cells, use=1):
     off_ref, w_ref, toff_ref, tw_ref = tables
-    groups, _, sets, per_set, _ = o_ref.shape
+    groups = o_ref.shape[0]
+    per_set = turn_ref.shape[2] // groups
+    sets = o_ref.shape[2] // per_set
     rows = 2 * half
     per_slab = 128 // cells
     first_row = lax.axis_index("band") * rows
@@ -135,7 +136,7 @@
         for g in range(sets):
             turn_ref[g, i * cells : (i + 1) * cells, :] = values[g]
     for g in range(sets):
-        o_ref[:, slab, g] = columns_first(turn_ref[g], groups)
+        o_ref[:, slab, g * per_set : (g + 1) * per_set] = columns_first(turn_ref[g], groups)
 
 
 def edge_kernel(cells, levels, half, far, x_ref, off_ref, w_ref, o_ref, turn_ref, ext_ref):
@@ -149,7 +150,7 @@
     cells, levels, half, x_ref, far_ref, near_ref, halo_ref, off_ref, w_ref, toff_ref, tw_ref, o_ref, mid_ref, own_ref, turn_ref, ext_ref
 ):
     level, core = here(levels)
-    sets = x_ref.shape[2]
+    sets = turn_ref.shape[0]
     row = core * half + 128 // cells
     first_pass(x_ref, 1, row, level, off_ref, w_ref, mid_ref, turn_ref, ext_ref, cells)
     for g in range(sets):
@@ -167,7 +168,7 @@
     cells, levels, half, edge_ref, mid_ref, halo_ref, off_ref, w_ref, toff_ref, tw_ref, i_ref, o_ref, own_ref, turn_ref, ext_ref
 ):
     level, core = here(levels)
-    for g in range(o_ref.shape[2]):
+    for g in range(turn_ref.shape[0]):
         part = slice(g * 128, (g + 1) * 128)
         own_ref[g, pl.ds(pl.multiple_of(core * 256, 128), 128), :] = halo_ref[part, :]
         own_ref[g, 128:256, :] = edge_ref[part, :]
@@ -198,7 +199,7 @@
     hspec = pl.BlockSpec(memory_space=pltpu.HBM)
     tables = (lon_offset.T, lon_weights.transpose(0, 2, 1), lat_offset.T, lat_weights.transpose(0, 2, 1))
     assert slabs == 3 and REACH * cells == 128 and columns == 128
-    sent = jax.ShapeDtypeStruct((groups // 2, 2, slabs, sets, per_set, 128), f32)
+    sent = jax.ShapeDtypeStruct((groups // 2, 2, slabs, sets * per_set, 128), f32)
     slab_lines = jax.ShapeDtypeStruct((sets * 128, 128), f32)
     gathered_shape = (groups, *sent.shape[2:])
     turn = VMEM((sets, 128, 128), f32)

time: 91.6 us -> 91.6 us (level)
  no operation moved by 1% of the time
where the time goes in v1:
time: 91.6 us; the launch traced here: 91.4 us
  blocking collectives  82.7 us (90%)
  Pallas kernels  3.75 us (4%)
  waiting for transfers between devices  2.97 us (3%)
  starting transfers between devices  1.92 us (2%)
    all_to_all x2, blocking collectives, exchanged(): return lax.all_to_all(x, 'lon', 0, 0, tiled=True)  80.2 us
    ppermute x1, waiting for transfers between devices, per_device(): far_halo = lax.ppermute(far, ('band', 'lon'), pairs)  2.97 us
    pallas_call x5, Pallas kernels, call(): pl.pallas_call(kernel, out_shape=out_shape, in_specs=in_specs, out_specs=...  2.86 us
    all_gather x1, blocking collectives, per_device(): lax.all_gather(near, 'lon', axis_index_groups=[[lon, lon + 1] for lon in...  2.47 us
    ppermute x1, starting transfers between devices, per_device(): far_halo = lax.ppermute(far, ('band', 'lon'), pairs)  1.92 us
  transfers between devices with their start and end apart: 1, of which 1 were waited for; matrix products, arithmetic and copies ran while one was open for 0% of the time, Pallas kernels for 1%

profile of v1, /device:TPU:25, one launch (start us, length us, event | category | flops | bytes accessed | tf_op | source)
XLA Modules:
  0.0 91.4 jit_solution(12315574696414445594)
XLA Ops:
  0.0 1.2 %shard_map.55 = (f32[32,2,3,4,128]{4,3,2,1,0:T(4,128)S(1)}, s32[4,48]{1,0:T(4,128)S(4)}, f32[4,4,48]{2,1,0:T(4,128)S(4)}, s32[4,48]{1,0:T(4,128)S(4)}, f32[4,4,48]{2,1,0:T(4,128)S(4)}) custom-call(f32[768,128]{1,0:T(8,128)} %bitcast.12, s32[4,48]{1,0:T(4,128)} %bitcast.15, f32[4,4,48]{2,1,0:T(4,128)} %bitcast.13, s32[4,48]{1,0:T(4,128)} %bitcast.16, ...), custom_call_target="tpu_custom_call" | custom-call | tf_op jit(solution)/shard_map/pallas_call | solution.py:210
  1.3 47.4 %all_to_all.10.x_ref = f32[64,3,4,128]{3,2,1,0:T(4,128)S(1)} all-to-all(f32[64,3,4,128]{3,2,1,0:T(4,128)S(1)} %bitcast.11), channel_id=1, replica_groups=mesh['band'=8,'lon'=64] {'lon'}, dimensions={0} | all-to-all | bytes 786432 | tf_op jit(solution)/shard_map/all_to_all | solution.py:183
  48.6 0.2 shard_map.56.far_ref.edge_ref
  48.9 1.9 %collective-permute-start = (f32[256,128]{1,0:T(8,128)S(1)}, f32[256,128]{1,0:T(8,128)S(1)}, u32[]{:S(2)}, u32[]{:S(2)}) collective-permute-start(f32[256,128]{1,0:T(8,128)S(1)} %shard_map.56.far_ref.edge_ref), channel_id=1, source_target_pairs={{1,64},{64,1},{3,66},{66,3},{5,68},{68,5},{7,70},{70,7},{9,72},{72... | collective-permute-start | bytes 393224 | tf_op jit(solution)/shard_map/ppermute | solution.py:241
  50.8 0.3 shard_map.57.near_ref
  51.1 2.5 %all-gather = f32[512,128]{1,0:T(8,128)S(1)} all-gather(f32[256,128]{1,0:T(8,128)S(1)} %shard_map.57.near_ref), channel_id=2, replica_groups={{0,1},{2,3},{4,5},{6,7},{8,9},{10,11},{12,13},{14,15},{16,17},{18,19},{..., dimensions={0}, use_global_device_ids=true | all-gather | bytes 393216 | tf_op jit(solution)/shard_map/all_gather | solution.py:243
  53.5 0.8 shard_map.58
  54.3 3.0 %collective-permute-done.halo_ref = f32[256,128]{1,0:T(8,128)S(1)} collective-permute-done((f32[256,128]{1,0:T(8,128)S(1)}, f32[256,128]{1,0:T(8,128)S(1)}, u32[]{:S(2)}, u32[]{:S(2)}) %collective-permute-start) | collective-permute-done | bytes 131104 | tf_op jit(solution)/shard_map/ppermute | solution.py:241
  57.3 0.4 shard_map.59
  57.7 32.8 %all_to_all.11 = f32[64,3,4,128]{3,2,1,0:T(4,128)S(1)} all-to-all(f32[64,3,4,128]{3,2,1,0:T(4,128)S(1)} %shard_map.59), channel_id=1, replica_groups=mesh['band'=8,'lon'=64] {'lon'}, dimensions={0} | all-to-all | bytes 786432 | tf_op jit(solution)/shard_map/all_to_all | solution.py:183
  90.5 0.9 last.1
Async XLA Ops:
  48.9 8.4 %collective-permute-start = (f32[256,128]{1,0:T(8,128)S(1)}, f32[256,128]{1,0:T(8,128)S(1)}, u32[]{:S(2)}, u32[]{:S(2)}) collective-permute-start(f32[256,128]{1,0:T(8,128)S(1)} %shard_map.56.far_ref.edge_ref), channel_id=1, source_target_pairs={{1,64},{64,1},{3,66},{66,3},{5,68},{68,5},{7,70},{70,7},{9,72},{72... | collective-permute-start | bytes 393224 | tf_op jit(solution)/shard_map/ppermute | solution.py:241

commit v2 on v1

--- a/solution.py
+++ b/solution.py
@@ -106,27 +106,26 @@
             o_ref[g * 128 + i * cells : g * 128 + (i + 1) * cells, :] = values[g]
 
 
-def rows_done(slab, half, window_ref, first_place, level, core, tables, o_ref, turn_ref, ext_ref, cells, use=1):
+def rows_done(slab, half, window_ref, base, level, core, tables, o_ref, turn_ref, ext_ref, cells, use=1):
     off_ref, w_ref, toff_ref, tw_ref = tables
     groups = o_ref.shape[0]
     per_set = turn_ref.shape[2] // groups
     sets = o_ref.shape[2] // per_set
     rows = 2 * half
     per_slab = 128 // cells
-    first_row = lax.axis_index("band") * rows
-    last_row = lax.axis_size("band") * rows - 1
-    half_row = core * half
-    first = half_row + slab * per_slab
+    first = core * half + slab * per_slab
+    origin = (lax.axis_index("band") * rows + first - base) * cells
+    end = (lax.axis_size("band") * rows - 1) * cells - origin
     exts = [[ext_ref[use * per_slab + i].at[g] for g in range(sets)] for i in range(per_slab)]
     starts = []
     for i in range(per_slab):
         row = first + i
-        shift = toff_ref[level, row]
+        shift = toff_ref[level, row] * cells
         totals = [None] * sets
         for k in range(4):
-            source = jnp.clip(first_row + row + (k - 1) - shift, 0, last_row) - first_row - half_row - first_place
+            source = jnp.minimum(jnp.maximum((base + i + k - 1) * cells - shift, -origin), end)
             weight = tw_ref[k, level, row]
-            where = pl.ds(pl.multiple_of(source * cells, cells), cells)
+            where = pl.ds(pl.multiple_of(source, cells), cells)
             for g in range(sets):
                 term = weight * window_ref[g, where, :]
                 totals[g] = term if totals[g] is None else totals[g] + term
@@ -161,7 +160,7 @@
         own_ref[g, pl.ds(pl.multiple_of(512 - core * 512, 128), 128), :] = halo_ref[1 - core, part, :]
     tables = (off_ref, w_ref, toff_ref, tw_ref)
     for use, slab in ((1, 1), (2, 2 - 2 * core)):
-        rows_done(slab, half, own_ref, -(128 // cells), level, core, tables, o_ref, turn_ref, ext_ref, cells, use)
+        rows_done(slab, half, own_ref, (slab + 1) * (128 // cells), level, core, tables, o_ref, turn_ref, ext_ref, cells, use)
 
 
 def outer_kernel(
@@ -174,9 +173,8 @@
         own_ref[g, 128:256, :] = edge_ref[part, :]
         own_ref[g, pl.ds(pl.multiple_of((1 - core) * 256, 128), 128), :] = mid_ref[part, :]
     slab = core * 2
-    first_place = (slab - 1) * (128 // cells)
     tables = (off_ref, w_ref, toff_ref, tw_ref)
-    rows_done(slab, half, own_ref, first_place, level, core, tables, o_ref, turn_ref, ext_ref, cells)
+    rows_done(slab, half, own_ref, 128 // cells, level, core, tables, o_ref, turn_ref, ext_ref, cells)
 
 
 def exchanged(x):

time: 91.6 us -> 91.6 us (level)
  no operation moved by 1% of the time
where the time goes in v2:
time: 91.6 us; the launch traced here: 91.3 us
  blocking collectives  82.7 us (90%)
  Pallas kernels  3.63 us (4%)
  waiting for transfers between devices  3.05 us (3%)
  starting transfers between devices  1.92 us (2%)
    all_to_all x2, blocking collectives, exchanged(): return lax.all_to_all(x, 'lon', 0, 0, tiled=True)  80.2 us
    ppermute x1, waiting for transfers between devices, per_device(): far_halo = lax.ppermute(far, ('band', 'lon'), pairs)  3.05 us
    pallas_call x5, Pallas kernels, call(): pl.pallas_call(kernel, out_shape=out_shape, in_specs=in_specs, out_specs=...  2.74 us
    all_gather x1, blocking collectives, per_device(): lax.all_gather(near, 'lon', axis_index_groups=[[lon, lon + 1] for lon in...  2.47 us
    ppermute x1, starting transfers between devices, per_device(): far_halo = lax.ppermute(far, ('band', 'lon'), pairs)  1.92 us
  transfers between devices with their start and end apart: 1, of which 1 were waited for; matrix products, arithmetic and copies ran while one was open for 0% of the time, Pallas kernels for 1%

profile of v2, /device:TPU:25, one launch (start us, length us, event | category | flops | bytes accessed | tf_op | source)
XLA Modules:
  0.0 91.3 jit_solution(5200057571835019397)
XLA Ops:
  0.0 1.2 %shard_map.55 = (f32[32,2,3,4,128]{4,3,2,1,0:T(4,128)S(1)}, s32[4,48]{1,0:T(4,128)S(4)}, f32[4,4,48]{2,1,0:T(4,128)S(4)}, s32[4,48]{1,0:T(4,128)S(4)}, f32[4,4,48]{2,1,0:T(4,128)S(4)}) custom-call(f32[768,128]{1,0:T(8,128)} %bitcast.12, s32[4,48]{1,0:T(4,128)} %bitcast.15, f32[4,4,48]{2,1,0:T(4,128)} %bitcast.13, s32[4,48]{1,0:T(4,128)} %bitcast.16, ...), custom_call_target="tpu_custom_call" | custom-call | tf_op jit(solution)/shard_map/pallas_call | solution.py:208
  1.3 47.4 %all_to_all.10.x_ref = f32[64,3,4,128]{3,2,1,0:T(4,128)S(1)} all-to-all(f32[64,3,4,128]{3,2,1,0:T(4,128)S(1)} %bitcast.11), channel_id=1, replica_groups=mesh['band'=8,'lon'=64] {'lon'}, dimensions={0} | all-to-all | bytes 786432 | tf_op jit(solution)/shard_map/all_to_all | solution.py:181
  48.6 0.2 shard_map.56.far_ref.edge_ref
  48.9 1.9 %collective-permute-start = (f32[256,128]{1,0:T(8,128)S(1)}, f32[256,128]{1,0:T(8,128)S(1)}, u32[]{:S(2)}, u32[]{:S(2)}) collective-permute-start(f32[256,128]{1,0:T(8,128)S(1)} %shard_map.56.far_ref.edge_ref), channel_id=1, source_target_pairs={{1,64},{64,1},{3,66},{66,3},{5,68},{68,5},{7,70},{70,7},{9,72},{72... | collective-permute-start | bytes 393224 | tf_op jit(solution)/shard_map/ppermute | solution.py:239
  50.8 0.3 shard_map.57.near_ref
  51.1 2.5 %all-gather = f32[512,128]{1,0:T(8,128)S(1)} all-gather(f32[256,128]{1,0:T(8,128)S(1)} %shard_map.57.near_ref), channel_id=2, replica_groups={{0,1},{2,3},{4,5},{6,7},{8,9},{10,11},{12,13},{14,15},{16,17},{18,19},{..., dimensions={0}, use_global_device_ids=true | all-gather | bytes 393216 | tf_op jit(solution)/shard_map/all_gather | solution.py:241
  53.5 0.7 shard_map.58
  54.2 3.0 %collective-permute-done.halo_ref = f32[256,128]{1,0:T(8,128)S(1)} collective-permute-done((f32[256,128]{1,0:T(8,128)S(1)}, f32[256,128]{1,0:T(8,128)S(1)}, u32[]{:S(2)}, u32[]{:S(2)}) %collective-permute-start) | collective-permute-done | bytes 131104 | tf_op jit(solution)/shard_map/ppermute | solution.py:239
  57.3 0.3 shard_map.59
  57.6 32.8 %all_to_all.11 = f32[64,3,4,128]{3,2,1,0:T(4,128)S(1)} all-to-all(f32[64,3,4,128]{3,2,1,0:T(4,128)S(1)} %shard_map.59), channel_id=1, replica_groups=mesh['band'=8,'lon'=64] {'lon'}, dimensions={0} | all-to-all | bytes 786432 | tf_op jit(solution)/shard_map/all_to_all | solution.py:181
  90.4 0.9 last.1
Async XLA Ops:
  48.9 8.4 %collective-permute-start = (f32[256,128]{1,0:T(8,128)S(1)}, f32[256,128]{1,0:T(8,128)S(1)}, u32[]{:S(2)}, u32[]{:S(2)}) collective-permute-start(f32[256,128]{1,0:T(8,128)S(1)} %shard_map.56.far_ref.edge_ref), channel_id=1, source_target_pairs={{1,64},{64,1},{3,66},{66,3},{5,68},{68,5},{7,70},{70,7},{9,72},{72... | collective-permute-start | bytes 393224 | tf_op jit(solution)/shard_map/ppermute | solution.py:239

commit v3 on v2

--- a/solution.py
+++ b/solution.py
@@ -61,16 +61,14 @@
 
 def placed(lines, offset, ext_refs, cells, lanes_per_block):
     lanes = lines[0].shape[1]
-    circle = lanes // lanes_per_block * cells
-    wrapped = offset & (circle - 1)
-    step = (wrapped >> (cells.bit_length() - 1)) * lanes_per_block
+    step = (offset >> (cells // lanes_per_block).bit_length() - 1) & (lanes - lanes_per_block)
     before = (step + lanes_per_block) & (lanes - 1)
     after = (step + lanes - lanes_per_block) & (lanes - 1)
     for line, ext_ref in zip(lines, ext_refs):
         ext_ref[0:cells] = pltpu.roll(line, before, 1)
         ext_ref[cells : 2 * cells] = pltpu.roll(line, step, 1)
         ext_ref[2 * cells : 2 * cells + 8] = pltpu.roll(line[0:8], after, 1)
-    return cells - 1 - (wrapped & (cells - 1))
+    return cells - 1 - (offset & (cells - 1))
 
 
 def tapped(start, weights, ext_refs, cells):

time: 91.6 us -> 91.5 us (level)
  no operation moved by 1% of the time
where the time goes in v3:
time: 91.5 us; the launch traced here: 91.3 us
  blocking collectives  82.7 us (90%)
  Pallas kernels  3.61 us (4%)
  waiting for transfers between devices  3.06 us (3%)
  starting transfers between devices  1.92 us (2%)
    all_to_all x2, blocking collectives, exchanged(): return lax.all_to_all(x, 'lon', 0, 0, tiled=True)  80.2 us
    ppermute x1, waiting for transfers between devices, per_device(): far_halo = lax.ppermute(far, ('band', 'lon'), pairs)  3.06 us
    pallas_call x5, Pallas kernels, call(): pl.pallas_call(kernel, out_shape=out_shape, in_specs=in_specs, out_specs=...  2.73 us
    all_gather x1, blocking collectives, per_device(): lax.all_gather(near, 'lon', axis_index_groups=[[lon, lon + 1] for lon in...  2.47 us
    ppermute x1, starting transfers between devices, per_device(): far_halo = lax.ppermute(far, ('band', 'lon'), pairs)  1.92 us
  transfers between devices with their start and end apart: 1, of which 1 were waited for; matrix products, arithmetic and copies ran while one was open for 0% of the time, Pallas kernels for 1%

profile of v3, /device:TPU:25, one launch (start us, length us, event | category | flops | bytes accessed | tf_op | source)
XLA Modules:
  0.0 91.3 jit_solution(3151426524211283585)
XLA Ops:
  0.0 1.2 %shard_map.55 = (f32[32,2,3,4,128]{4,3,2,1,0:T(4,128)S(1)}, s32[4,48]{1,0:T(4,128)S(4)}, f32[4,4,48]{2,1,0:T(4,128)S(4)}, s32[4,48]{1,0:T(4,128)S(4)}, f32[4,4,48]{2,1,0:T(4,128)S(4)}) custom-call(f32[768,128]{1,0:T(8,128)} %bitcast.12, s32[4,48]{1,0:T(4,128)} %bitcast.15, f32[4,4,48]{2,1,0:T(4,128)} %bitcast.13, s32[4,48]{1,0:T(4,128)} %bitcast.16, ...), custom_call_target="tpu_custom_call" | custom-call | tf_op jit(solution)/shard_map/pallas_call | solution.py:206
  1.3 47.4 %all_to_all.10.x_ref = f32[64,3,4,128]{3,2,1,0:T(4,128)S(1)} all-to-all(f32[64,3,4,128]{3,2,1,0:T(4,128)S(1)} %bitcast.11), channel_id=1, replica_groups=mesh['band'=8,'lon'=64] {'lon'}, dimensions={0} | all-to-all | bytes 786432 | tf_op jit(solution)/shard_map/all_to_all | solution.py:179
  48.6 0.2 shard_map.56.far_ref.edge_ref
  48.9 1.9 %collective-permute-start = (f32[256,128]{1,0:T(8,128)S(1)}, f32[256,128]{1,0:T(8,128)S(1)}, u32[]{:S(2)}, u32[]{:S(2)}) collective-permute-start(f32[256,128]{1,0:T(8,128)S(1)} %shard_map.56.far_ref.edge_ref), channel_id=1, source_target_pairs={{1,64},{64,1},{3,66},{66,3},{5,68},{68,5},{7,70},{70,7},{9,72},{72... | collective-permute-start | bytes 393224 | tf_op jit(solution)/shard_map/ppermute | solution.py:237
  50.8 0.3 shard_map.57.near_ref
  51.1 2.5 %all-gather = f32[512,128]{1,0:T(8,128)S(1)} all-gather(f32[256,128]{1,0:T(8,128)S(1)} %shard_map.57.near_ref), channel_id=2, replica_groups={{0,1},{2,3},{4,5},{6,7},{8,9},{10,11},{12,13},{14,15},{16,17},{18,19},{..., dimensions={0}, use_global_device_ids=true | all-gather | bytes 393216 | tf_op jit(solution)/shard_map/all_gather | solution.py:239
  53.5 0.7 shard_map.58
  54.2 3.1 %collective-permute-done.halo_ref = f32[256,128]{1,0:T(8,128)S(1)} collective-permute-done((f32[256,128]{1,0:T(8,128)S(1)}, f32[256,128]{1,0:T(8,128)S(1)}, u32[]{:S(2)}, u32[]{:S(2)}) %collective-permute-start) | collective-permute-done | bytes 131104 | tf_op jit(solution)/shard_map/ppermute | solution.py:237
  57.3 0.3 shard_map.59
  57.6 32.8 %all_to_all.11 = f32[64,3,4,128]{3,2,1,0:T(4,128)S(1)} all-to-all(f32[64,3,4,128]{3,2,1,0:T(4,128)S(1)} %shard_map.59), channel_id=1, replica_groups=mesh['band'=8,'lon'=64] {'lon'}, dimensions={0} | all-to-all | bytes 786432 | tf_op jit(solution)/shard_map/all_to_all | solution.py:179
  90.4 0.9 last.1
Async XLA Ops:
  48.9 8.4 %collective-permute-start = (f32[256,128]{1,0:T(8,128)S(1)}, f32[256,128]{1,0:T(8,128)S(1)}, u32[]{:S(2)}, u32[]{:S(2)}) collective-permute-start(f32[256,128]{1,0:T(8,128)S(1)} %shard_map.56.far_ref.edge_ref), channel_id=1, source_target_pairs={{1,64},{64,1},{3,66},{66,3},{5,68},{68,5},{7,70},{70,7},{9,72},{72... | collective-permute-start | bytes 393224 | tf_op jit(solution)/shard_map/ppermute | solution.py:237
